TPU v7x, 512 devices: a whole 4x8x8 slice. The times are simulated.
512 devices in a mesh: leaf: 8 (over z), row: 4 (over x), col: 16 (over y, core).
Axes of the slice: x: 4, y: 8, z: 8, core: 2. Of those that a mesh axis runs over, the one named last changes fastest.
Arguments:
- leaf_rhs: float32 [16, 16, 4096], P('leaf', None, 'col'), may hold values from -6 to 6
- leaf_inverse: float32 [16, 4096, 4096], P('leaf', 'row', 'col'), as said below
- update_rows: float32 [16, 2048, 4096], P('leaf', 'col', 'row'), may hold values from -0.09375 to 0.09375
- update_map: int32 [16, 16], P('leaf'), may hold values from 0 to 31, as said below
- sep_rhs: float32 [16, 4096], replicated, may hold values from -6 to 6
- sep_inverse: float32 [4096, 4096], P(('leaf', 'row', 'col')), as said below
Outputs:
- leaf_solution: float32 [16, 16, 4096], P('leaf', None, ('col', 'row'))
- sep_solution: float32 [16, 4096], P(None, ('leaf', 'row', 'col'))
Inputs may be any that keep to these rules, and one draw needn't show every extreme that they name: `update_map`: each row names 16 different separator blocks. `leaf_inverse`: entries off the diagonal are independent and of order 1 / sqrt(4096); each diagonal entry is one plus such a term. `sep_inverse`: entries off the diagonal are independent and of order 1 / sqrt(4096); each diagonal entry is one plus such a term.
All inputs are finite; a program needn't handle non-finite values.
Results may differ from a plain program's by a relative error of at most 0.000068.
Values sent between devices are 32-bit elements; how exact they have to be, the bound alone decides.
A program may use at most 64 MiB of HBM per device.

v0:
```python
import jax
import jax.numpy as jnp
from jax import lax
from jax.sharding import PartitionSpec as P

BLOCK = 128
HIGH = lax.Precision.HIGHEST


def body(leaf_rhs, leaf_inverse, update_rows, update_map, sep_rhs, sep_inverse):
    subs = leaf_rhs.shape[0]
    nrhs = leaf_rhs.shape[1]
    width = sep_rhs.shape[1]
    blocks_total = width // BLOCK
    blocks_here = update_rows.shape[1] // BLOCK
    first_block = lax.axis_index("col") * blocks_here
    local_map = lax.dynamic_slice_in_dim(update_map, first_block, blocks_here, 1)
    onehot = (
        local_map[:, :, None] == jnp.arange(blocks_total, dtype=jnp.int32)[None, None, :]
    ).astype(jnp.float32)
    partial_fwd = jnp.einsum("sij,srj->sri", leaf_inverse, leaf_rhs, precision=HIGH)
    forward = lax.psum(partial_fwd, "col")
    coupled = jnp.einsum("sun,srn->sru", update_rows, forward, precision=HIGH)
    coupled = coupled.reshape(subs, nrhs, blocks_here, BLOCK)
    contrib = jnp.einsum("srkc,skb->rbc", coupled, onehot, precision=HIGH).reshape(nrhs, width)
    sep_rows = sep_inverse.shape[0]
    row_start = lax.axis_index(("leaf", "row", "col")) * sep_rows
    total = lax.psum(contrib, ("leaf", "row", "col"))
    updated = sep_rhs - total
    sep_forward = jnp.einsum("ij,rj->ri", sep_inverse, updated, precision=HIGH)
    back_terms = jnp.einsum("ij,ri->rj", sep_inverse, sep_forward, precision=HIGH)
    sep_whole = lax.psum(back_terms, ("leaf", "row", "col"))
    sep_solution = lax.dynamic_slice_in_dim(sep_whole, row_start, sep_rows, 1)
    pulled = jnp.einsum(
        "rbc,skb->srkc", sep_whole.reshape(nrhs, blocks_total, BLOCK), onehot, precision=HIGH
    )
    pulled = pulled.reshape(subs, nrhs, blocks_here * BLOCK)
    pull_terms = jnp.einsum("sun,sru->srn", update_rows, pulled, precision=HIGH)
    pull_total = lax.psum(pull_terms, "col")
    reduced = forward - pull_total
    column_terms = jnp.einsum("sij,sri->srj", leaf_inverse, reduced, precision=HIGH)
    leaf_solution = lax.psum_scatter(column_terms, "row", scatter_dimension=2, tiled=True)
    return (leaf_solution, sep_solution)


def solution(mesh):
    in_specs = (
        P("leaf", None, "col"),
        P("leaf", "row", "col"),
        P("leaf", "col", "row"),
        P("leaf", None),
        P(),
        P(("leaf", "row", "col"), None),
    )
    out_specs = (P("leaf", None, ("col", "row")), P(None, ("leaf", "row", "col")))
    return jax.shard_map(body, mesh=mesh, in_specs=in_specs, out_specs=out_specs, check_vma=False)
```

profile of v0, /device:TPU:8, one launch (start us, length us, event | category | flops | bytes accessed | tf_op | source)
XLA Modules:
  0.0 833.5 jit_solution(7228872072157452738)
XLA Ops:
  7.2 0.0 all-reduce.5.cloned.1.call-start
  7.3 1.5 copy-done
  8.8 3.2 fusion.17
  12.0 0.0 all-reduce.5.cloned.1.call-update
  12.0 0.0 all-reduce.7.cloned.1.call-start
  12.1 0.2 dynamic-slice_reduce_fusion
  12.3 117.6 %all-reduce.5.cloned.1.call-done = f32[2,16,1024]{2,1,0:T(8,128)} async-done(((f32[2,16,1024]{2,1,0:T(8,128)}), f32[2,16,1024]{2,1,0:T(8,128)}) %all-reduce.5.cloned.1.call-update) | async-done | bytes 131088 | tf_op jit(solution)/shard_map/psum | solution.py:22
  129.9 1.9 fusion.18
  131.8 0.4 fusion.6
  132.2 0.9 copy.21
  133.1 0.0 all-reduce.7.cloned.1.call-update
  133.1 0.0 all-reduce.9.cloned.1.call-start
  133.2 275.3 %all-reduce.7.cloned.1.call-done = f32[16,4096]{1,0:T(8,128)} async-done(((f32[16,4096]{1,0:T(8,128)}), f32[16,4096]{1,0:T(8,128)}) %all-reduce.7.cloned.1.call-update) | async-done | bytes 262160 | tf_op jit(solution)/shard_map/psum | solution.py:28
  408.4 1.5 fusion
  409.9 1.1 fusion.19
  411.0 0.0 all-reduce.9.cloned.1.call-update
  411.0 0.0 all-reduce.11.cloned.1.call-start
  411.1 270.1 %all-reduce.9.cloned.1.call-done = f32[16,4096]{1,0:T(8,128)} async-done(((f32[16,4096]{1,0:T(8,128)}), f32[16,4096]{1,0:T(8,128)}) %all-reduce.9.cloned.1.call-update) | async-done | bytes 262160 | tf_op jit(solution)/shard_map/psum | solution.py:32
  681.1 1.0 copy.15
  682.1 0.2 fusion.8
  682.4 1.3 fusion.4
  683.7 0.0 reduce-scatter.4.cloned.1.call-start
  683.7 110.0 %all-reduce.11.cloned.1.call-done = f32[2,16,1024]{2,1,0:T(8,128)} async-done(((f32[2,16,1024]{2,1,0:T(8,128)}), f32[2,16,1024]{2,1,0:T(8,128)}) %all-reduce.11.cloned.1.call-update) | async-done | bytes 131088 | tf_op jit(solution)/shard_map/psum | solution.py:39
  793.7 2.0 fusion.2
  795.7 0.1 copy.12
  795.9 0.9 reshape.76
  796.7 0.0 reduce-scatter.4.cloned.1.call-update
  796.8 0.8 constant_dynamic-slice_fusion
  797.6 0.7 copy.9
  798.2 27.2 %reduce-scatter.4.cloned.1.call-done = f32[64,32]{1,0:T(8,128)} async-done(((f32[256,32]{1,0:T(8,128)}), f32[64,32]{1,0:T(8,128)}) %reduce-scatter.4.cloned.1.call-update) | async-done | bytes 8208
  825.4 0.9 reshape.77
  826.3 0.7 copy.13
  (10 shorter events, 0.0 us)
Async XLA Ops:
  7.2 1.6 copy-start
  7.2 4.9 copy-start.4
  7.2 122.7 %copy-start.1 = (f32[2,128,1024]{2,1,0:T(8,128)S(1)}, f32[2,128,1024]{2,1,0:T(8,128)}, u32[]{:S(2)}) copy-start(f32[2,128,1024]{2,1,0:T(8,128)} %param.8) | copy-start | bytes 3145732
  7.2 401.2 %copy-start.3 = (f32[8,4096]{1,0:T(8,128)S(1)}, f32[8,4096]{1,0:T(8,128)}, u32[]{:S(2)}) copy-start(f32[8,4096]{1,0:T(8,128)} %param.11) | copy-start | bytes 393220
  7.2 122.7 %all-reduce.5.cloned.1.call-start = ((), (), s32[]{:S(2)}) async-start(), calls=%async_computation.1 | async-start | bytes 262144 | tf_op jit(solution)/shard_map/psum | solution.py:22
  12.0 396.4 %all-reduce.7.cloned.1.call-start = ((), (), s32[]{:S(2)}) async-start(), calls=%async_computation.2 | async-start | bytes 524288 | tf_op jit(solution)/shard_map/psum | solution.py:28
  132.2 661.5 %copy-start.2 = (f32[2,16,1024]{2,1,0:T(8,128)S(1)}, f32[2,16,1024]{2,1,0:T(8,128)}, u32[]{:S(2)}) copy-start(f32[2,16,1024]{2,1,0:T(8,128)} %all-reduce.5.cloned.1.call-done) | copy-start | bytes 393220
  133.1 548.0 %all-reduce.9.cloned.1.call-start = ((), (), s32[]{:S(2)}) async-start(), calls=%async_computation.3 | async-start | bytes 524288 | tf_op jit(solution)/shard_map/psum | solution.py:32
  411.0 382.7 %all-reduce.11.cloned.1.call-start = ((), (), s32[]{:S(2)}) async-start(), calls=%async_computation.4 | async-start | bytes 262144 | tf_op jit(solution)/shard_map/psum | solution.py:39
  683.7 141.8 %reduce-scatter.4.cloned.1.call-start = ((), (), s32[]{:S(2)}) async-start(), calls=%async_computation.5 | async-start | bytes 163840
Sparse Core Ops, SparseCore 0:
  12.1 117.7 all-reduce.4
  134.9 273.4 all-reduce.6
  413.4 267.6 all-reduce.8
  683.8 109.8 all-reduce.10
  796.9 28.5 reduce-scatter.3
where the time goes:
time: 834 us
  waiting for transfers between devices  800 us (96%)
  between operations  13.9 us (2%)
  matrix products  11.6 us (1%)
    psum x1, waiting for transfers between devices, body(): total = lax.psum(contrib, ('leaf', 'row', 'col'))  275 us
    psum x1, waiting for transfers between devices, body(): sep_whole = lax.psum(back_terms, ('leaf', 'row', 'col'))  270 us
    psum x1, waiting for transfers between devices, body(): forward = lax.psum(partial_fwd, 'col')  118 us
    psum x1, waiting for transfers between devices, body(): pull_total = lax.psum(pull_terms, 'col')  110 us
    unnamed x6, waiting for transfers between devices  27.3 us
  transfers between devices with their start and end apart: 5, of which 5 were waited for; matrix products, arithmetic and copies ran while one was open for 0% of the time, Pallas kernels for 0%

commit v1 on v0

--- a/solution.py
+++ b/solution.py
@@ -29,7 +29,9 @@
     updated = sep_rhs - total
     sep_forward = jnp.einsum("ij,rj->ri", sep_inverse, updated, precision=HIGH)
     back_terms = jnp.einsum("ij,ri->rj", sep_inverse, sep_forward, precision=HIGH)
-    sep_whole = lax.psum(back_terms, ("leaf", "row", "col"))
+    sep_whole = back_terms
+    for to_i in (("row", "col"), "leaf"):
+        sep_whole = lax.psum(sep_whole, to_i)
     sep_solution = lax.dynamic_slice_in_dim(sep_whole, row_start, sep_rows, 1)
     pulled = jnp.einsum(
         "rbc,skb->srkc", sep_whole.reshape(nrhs, blocks_total, BLOCK), onehot, precision=HIGH

time: 834 us -> 831 us (level)
    psum x1 -> x2, waiting for transfers between devices: 270 us -> 265 us  [body(): sep_whole = lax.psum(sep_whole, to_i)]
    unnamed x6 -> x7, waiting for transfers between devices: 27.3 us -> 27.3 us
  transfers between devices with their start and end apart: 5 -> 6, of which waited for: 5 -> 6; matrix products, arithmetic and copies ran while one was open for 0% -> 0% of each run, Pallas kernels for 0% -> 0%
where the time goes in v1:
time: 831 us; the launch traced here: 830 us
  waiting for transfers between devices  797 us (96%)
  between operations  14.2 us (2%)
  matrix products  11.6 us (1%)
    psum x1, waiting for transfers between devices, body(): total = lax.psum(contrib, ('leaf', 'row', 'col'))  275 us
    psum x2, waiting for transfers between devices, body(): sep_whole = lax.psum(sep_whole, to_i)  265 us
    psum x1, waiting for transfers between devices, body(): forward = lax.psum(partial_fwd, 'col')  118 us
    psum x1, waiting for transfers between devices, body(): pull_total = lax.psum(pull_terms, 'col')  111 us
    unnamed x7, waiting for transfers between devices  27.3 us
  transfers between devices with their start and end apart: 6, of which 6 were waited for; matrix products, arithmetic and copies ran while one was open for 0% of the time, Pallas kernels for 0%

profile of v1, /device:TPU:8, one launch (start us, length us, event | category | flops | bytes accessed | tf_op | source)
XLA Modules:
  0.0 830.4 jit_solution(17563032056601868439)
XLA Ops:
  7.2 0.0 all-reduce.6.cloned.1.call-start
  7.3 1.5 copy-done
  8.8 3.2 fusion.17
  12.0 0.0 all-reduce.6.cloned.1.call-update
  12.0 0.0 all-reduce.8.cloned.1.call-start
  12.1 0.2 dynamic-slice_reduce_fusion
  12.3 117.6 %all-reduce.6.cloned.1.call-done = f32[2,16,1024]{2,1,0:T(8,128)} async-done(((f32[2,16,1024]{2,1,0:T(8,128)}), f32[2,16,1024]{2,1,0:T(8,128)}) %all-reduce.6.cloned.1.call-update) | async-done | bytes 131088 | tf_op jit(solution)/shard_map/psum | solution.py:22
  129.9 1.9 fusion.18
  131.8 0.4 fusion.6
  132.2 0.9 copy.21
  133.1 0.0 all-reduce.8.cloned.1.call-update
  133.1 0.0 all-reduce.10.cloned.1.call-start
  133.1 275.3 %all-reduce.8.cloned.1.call-done = f32[16,4096]{1,0:T(8,128)} async-done(((f32[16,4096]{1,0:T(8,128)}), f32[16,4096]{1,0:T(8,128)}) %all-reduce.8.cloned.1.call-update) | async-done | bytes 262160 | tf_op jit(solution)/shard_map/psum | solution.py:28
  408.4 1.5 fusion
  409.9 1.1 fusion.19
  411.0 0.0 all-reduce.12.cloned.1.call-start
  411.0 184.7 %all-reduce.10.cloned.1.call-done = f32[16,4096]{1,0:T(8,128)} async-done(((f32[16,4096]{1,0:T(8,128)}), f32[16,4096]{1,0:T(8,128)}) %all-reduce.10.cloned.1.call-update) | async-done | bytes 262160 | tf_op jit(solution)/shard_map/psum | solution.py:34
  595.8 0.0 all-reduce.14.cloned.1.call-start
  595.8 80.5 %all-reduce.12.cloned.1.call-done = f32[16,4096]{1,0:T(8,128)} async-done(((f32[16,4096]{1,0:T(8,128)}), f32[16,4096]{1,0:T(8,128)}) %all-reduce.12.cloned.1.call-update) | async-done | bytes 262160 | tf_op jit(solution)/shard_map/psum | solution.py:34
  676.4 1.0 copy.15
  677.4 0.2 fusion.8
  677.6 1.3 fusion.4
  678.9 0.0 reduce-scatter.4.cloned.1.call-start
  679.0 111.4 %all-reduce.14.cloned.1.call-done = f32[2,16,1024]{2,1,0:T(8,128)} async-done(((f32[2,16,1024]{2,1,0:T(8,128)}), f32[2,16,1024]{2,1,0:T(8,128)}) %all-reduce.14.cloned.1.call-update) | async-done | bytes 131088 | tf_op jit(solution)/shard_map/psum | solution.py:41
  790.3 2.0 fusion.2
  792.3 0.1 copy.12
  792.5 0.9 reshape.76
  793.4 0.8 constant_dynamic-slice_fusion
  794.2 0.7 copy.9
  794.8 27.2 %reduce-scatter.4.cloned.1.call-done = f32[64,32]{1,0:T(8,128)} async-done(((f32[256,32]{1,0:T(8,128)}), f32[64,32]{1,0:T(8,128)}) %reduce-scatter.4.cloned.1.call-update) | async-done | bytes 8208
  822.1 0.9 reshape.77
  822.9 0.7 copy.13
  (13 shorter events, 0.1 us)
Async XLA Ops:
  7.2 1.6 copy-start
  7.2 4.9 copy-start.4
  7.2 122.7 %copy-start.1 = (f32[2,128,1024]{2,1,0:T(8,128)S(1)}, f32[2,128,1024]{2,1,0:T(8,128)}, u32[]{:S(2)}) copy-start(f32[2,128,1024]{2,1,0:T(8,128)} %param.8) | copy-start | bytes 3145732
  7.2 401.2 %copy-start.3 = (f32[8,4096]{1,0:T(8,128)S(1)}, f32[8,4096]{1,0:T(8,128)}, u32[]{:S(2)}) copy-start(f32[8,4096]{1,0:T(8,128)} %param.11) | copy-start | bytes 393220
  7.2 122.7 %all-reduce.6.cloned.1.call-start = ((), (), s32[]{:S(2)}) async-start(), calls=%async_computation.1 | async-start | bytes 262144 | tf_op jit(solution)/shard_map/psum | solution.py:22
  12.0 396.4 %all-reduce.8.cloned.1.call-start = ((), (), s32[]{:S(2)}) async-start(), calls=%async_computation.2 | async-start | bytes 524288 | tf_op jit(solution)/shard_map/psum | solution.py:28
  133.1 657.2 %copy-start.2 = (f32[2,16,1024]{2,1,0:T(8,128)S(1)}, f32[2,16,1024]{2,1,0:T(8,128)}, u32[]{:S(2)}) copy-start(f32[2,16,1024]{2,1,0:T(8,128)} %all-reduce.6.cloned.1.call-done) | copy-start | bytes 393220
  133.1 462.7 %all-reduce.10.cloned.1.call-start = ((), (), s32[]{:S(2)}) async-start(), calls=%async_computation.3 | async-start | bytes 524288 | tf_op jit(solution)/shard_map/psum | solution.py:34
  411.0 265.4 %all-reduce.12.cloned.1.call-start = ((), (), s32[]{:S(2)}) async-start(), calls=%async_computation.4 | async-start | bytes 524288 | tf_op jit(solution)/shard_map/psum | solution.py:34
  595.8 194.5 %all-reduce.14.cloned.1.call-start = ((), (), s32[]{:S(2)}) async-start(), calls=%async_computation.5 | async-start | bytes 262144 | tf_op jit(solution)/shard_map/psum | solution.py:41
  678.9 143.2 %reduce-scatter.4.cloned.1.call-start = ((), (), s32[]{:S(2)}) async-start(), calls=%async_computation.6 | async-start | bytes 163840
Sparse Core Ops, SparseCore 0:
  12.1 117.7 all-reduce.5
  134.9 273.4 all-reduce.7
  411.9 183.8 all-reduce.9
  597.9 78.3 all-reduce.11
  679.0 111.2 all-reduce.13
  793.5 28.5 reduce-scatter.3
